TPU v7x, 512 devices: a whole 4x4x16 slice. The times are simulated.
512 devices in a mesh: freq: 16 (over y, x_hi, core), gx: 32 (over z, x_lo).
Axes of the slice: x: 4 (x_hi: 2, x_lo: 2; x = x_hi * 2 + x_lo), y: 4, z: 16, core: 2. Of those that a mesh axis runs over, the one named last changes fastest.
Arguments:
- sigma_h: float32 [128, 64, 256], P('gx'), may hold values from 0.3 to 3
- sigma_v: float32 [128, 64, 256], P('gx'), may hold values from 0.3 to 3
- wave_scale: float32 [16], P('freq'), may hold values from 0.25 to 4
- field_start: bfloat16 [16, 2, 3, 128, 64, 256], P('freq', None, None, 'gx'), may hold values from -6 to 6
- adjoint_start: bfloat16 [16, 2, 3, 128, 64, 256], P('freq', None, None, 'gx'), may hold values from -6 to 6
- observed: bfloat16 [16, 2, 3, 128, 64, 256], P('freq', None, None, 'gx'), may hold values from -6 to 6
- tx_count: int32 [1], replicated, may hold values from 1 to 64
- tx_cells: int32 [64], replicated, may hold values from 0 to 2097151
Outputs:
- gradient: float32 [2, 128, 64, 256], P(None, 'gx', 'freq')
- final_field: float32 [16, 2, 3, 128, 64, 256], P('freq', None, None, 'gx')
All inputs are finite; a program needn't handle non-finite values.
Results may differ from a plain program's by a relative error of at most 0.0003.
Values sent between devices are 32-bit elements; how exact they have to be, the bound alone decides.
No kernel may reach another device: no remote copies, remote signals or barrier semaphores. Data moves between devices by JAX's collectives and lax.ppermute only.
A program may use at most 64 MiB of HBM per device.

v0:
```python
import jax
import jax.numpy as jnp
from jax import lax
from jax.sharding import PartitionSpec as P

ITERS = 2
THETA = 0.5
SOURCE_GAIN = 8.0


def padded_2(cells, sides, width):
    for axis, dim in sides:
        count = lax.axis_size(axis)
        ends = count - 1
        head = lax.slice_in_dim(cells, 0, width, axis=dim)
        tail = lax.slice_in_dim(cells, cells.shape[dim] - width, cells.shape[dim], axis=dim)
        cells = jnp.concatenate(
            [
                lax.ppermute(tail, axis, [(i, (i + 1) % count) for i in range(ends)]),
                cells,
                lax.ppermute(head, axis, [((i + 1) % count, i) for i in range(ends)]),
            ],
            axis=dim,
        )
    return cells


def ahead_diff(values, along):
    along = values.ndim + along
    widths = [(0, 0)] * values.ndim
    widths[along] = (0, 1)
    padded = jnp.pad(values, widths)
    return lax.slice_in_dim(padded, 1, values.shape[along] + 1, axis=along) - values


def behind_diff(values, along):
    along = values.ndim + along
    widths = [(0, 0)] * values.ndim
    widths[along] = (1, 0)
    padded = jnp.pad(values, widths)
    return values - lax.slice_in_dim(padded, 0, values.shape[along], axis=along)


def curl_masked(efield, inside):
    comp_x = efield[..., 0, :, :, :]
    comp_y = efield[..., 1, :, :, :]
    comp_z = efield[..., 2, :, :, :]
    twist_x = (ahead_diff(comp_z, -2) - ahead_diff(comp_y, -1)) * inside
    twist_y = (ahead_diff(comp_x, -1) - ahead_diff(comp_z, -3)) * inside
    twist_z = (ahead_diff(comp_y, -3) - ahead_diff(comp_x, -2)) * inside
    back_x = behind_diff(twist_z, -2) - behind_diff(twist_y, -1)
    back_y = behind_diff(twist_x, -1) - behind_diff(twist_z, -3)
    back_z = behind_diff(twist_y, -3) - behind_diff(twist_x, -2)
    return jnp.stack([back_x, back_y, back_z], axis=-4)


def relax(efield, curled, source_term, sig_pair, wave_scale):
    sigma_comp = jnp.stack([sig_pair[0], sig_pair[0], sig_pair[1]])
    coupling = wave_scale[:, None, None, None, None] * sigma_comp[None]
    real_part = efield[:, 0]
    imag_part = efield[:, 1]
    resid_real = source_term[:, 0] - (curled[:, 0] - coupling * imag_part)
    resid_imag = source_term[:, 1] - (curled[:, 1] + coupling * real_part)
    modulus = 16.0 + coupling * coupling
    update_real = (4.0 * resid_real + coupling * resid_imag) / modulus
    update_imag = (4.0 * resid_imag - coupling * resid_real) / modulus
    return efield + THETA * jnp.stack([update_real, update_imag], axis=1)


def make_source(tx_cells, tx_count, wave_scale, x_start, slab_width, size_y, size_z):
    plane_size = size_y * size_z
    cell_x = tx_cells // plane_size - x_start
    remainder = tx_cells % plane_size
    cell_y = remainder // size_z
    cell_z = remainder % size_z
    active = (jnp.arange(tx_cells.shape[0]) < tx_count[0]) & (cell_x >= 0) & (cell_x < slab_width)
    weights = jnp.where(active, 1.0, 0.0).astype(jnp.float32)
    counts = jnp.zeros((slab_width, size_y, size_z), jnp.float32)
    counts = counts.at[jnp.clip(cell_x, 0, slab_width - 1), cell_y, cell_z].add(weights)
    imag_x = SOURCE_GAIN * wave_scale[:, None, None, None] * counts[None]
    blank = jnp.zeros_like(imag_x)
    real_block = jnp.stack([blank, blank, blank], axis=1)
    imag_block = jnp.stack([imag_x, blank, blank], axis=1)
    return jnp.stack([real_block, imag_block], axis=1)


def adjoint_source(efield, observed):
    differ = efield - observed.astype(jnp.float32)
    return jnp.stack([differ[:, 0], -differ[:, 1]], axis=1)


def gradient_terms(efield, adjoint, wave_scale):
    product = adjoint[:, 0] * efield[:, 1] + adjoint[:, 1] * efield[:, 0]
    weighted = wave_scale[:, None, None, None, None] * product
    horizontal = jnp.sum(weighted[:, 0] + weighted[:, 1], axis=0)
    vertical = jnp.sum(weighted[:, 2], axis=0)
    return jnp.stack([horizontal, vertical])


def inside_mask(first, width, total_x):
    positions = first + jnp.arange(width)
    return ((positions >= 0) & (positions < total_x)).astype(jnp.float32)[:, None, None]


def local_sweep(efield, source_term, sig_pair, wave_scale, inside_pad):
    padded = padded_2(efield, (("gx", 3),), 1)
    curled = curl_masked(padded, inside_pad)[:, :, :, 1:-1]
    return relax(efield, curled, source_term, sig_pair, wave_scale)


def on_device(
    sigma_h, sigma_v, wave_scale, field_start, adjoint_start, observed, tx_count, tx_cells
):
    slab_width = sigma_h.shape[0]
    size_y = sigma_h.shape[1]
    size_z = sigma_h.shape[2]
    slab_index = lax.axis_index("gx")
    total_x = slab_width * lax.axis_size("gx")
    slab_first = slab_index * slab_width
    sig_pair = jnp.stack([sigma_h, sigma_v])
    efield = field_start.astype(jnp.float32)
    adjoint = adjoint_start.astype(jnp.float32)
    inside_pad = inside_mask(slab_first - 1, slab_width + 2, total_x)
    source_term = make_source(
        tx_cells, tx_count, wave_scale, slab_first, slab_width, size_y, size_z
    )
    for sweep in range(ITERS):
        efield = local_sweep(efield, source_term, sig_pair, wave_scale, inside_pad)
    adjoint_rhs = adjoint_source(efield, observed)
    for sweep in range(ITERS):
        adjoint = local_sweep(adjoint, adjoint_rhs, sig_pair, wave_scale, inside_pad)
    local_grad = gradient_terms(efield, adjoint, wave_scale)
    summed = lax.psum(local_grad, "freq")
    share_rows = size_y // lax.axis_size("freq")
    gradient = lax.dynamic_slice_in_dim(summed, lax.axis_index("freq") * share_rows, share_rows, 2)
    return (gradient, efield)


def solution(mesh):
    placed = (
        P("gx", None, None),
        P("gx", None, None),
        P("freq"),
        P("freq", None, None, "gx", None, None),
        P("freq", None, None, "gx", None, None),
        P("freq", None, None, "gx", None, None),
        P(),
        P(),
    )
    return jax.shard_map(
        on_device,
        mesh=mesh,
        in_specs=placed,
        out_specs=(P(None, "gx", "freq", None), P("freq", None, None, "gx", None, None)),
        check_vma=False,
    )
```

profile of v0, /device:TPU:1, one launch (start us, length us, event | category | flops | bytes accessed | tf_op | source)
XLA Modules:
  0.0 269.4 jit_solution(7268834031824373260)
XLA Ops:
  7.2 1.2 fusion.149
  8.4 0.8 copy.50
  9.2 4.7 %collective-permute-start = (f32[1,2,3,1,64,256]{5,4,3,1,2,0:T(8,128)}, f32[1,2,3,1,64,256]{5,4,3,1,2,0:T(8,128)}, u32[]{:S(2)}, u32[]{:S(2)}) collective-permute-start(f32[1,2,3,1,64,256]{5,4,3,1,2,0:T(8,128)} %copy.50), channel_id=1, source_target_pairs={{0,1},{1,2},{2,3},{3,4},{4,5},{5,6},{6,7},{7,8},{8,9},{9,10},{10,1... | collective-permute-start | bytes 1179656 | tf_op jit(solution)/shard_map/ppermute | solution.py:19
  13.9 0.8 copy.51
  14.7 1.4 collective-permute-start.1
  16.3 1.0 fusion.147
  17.3 4.7 %collective-permute-start.4 = (f32[1,2,3,1,64,256]{5,4,3,1,2,0:T(8,128)}, f32[1,2,3,1,64,256]{5,4,3,1,2,0:T(8,128)}, u32[]{:S(2)}, u32[]{:S(2)}) collective-permute-start(f32[1,2,3,1,64,256]{5,4,3,1,2,0:T(8,128)} %get-tuple-element.30), channel_id=1, source_target_pairs={{0,1},{1,2},{2,3},{3,4},{4,5},{5,6},{6,7},{7,8},{8,9},{9,10},{10,1... | collective-permute-start | bytes 1179656 | tf_op jit(solution)/shard_map/ppermute | solution.py:19
  22.0 1.3 collective-permute-start.5
  24.0 1.3 convert_element_type.71
  26.0 4.6 %scatter_fusion = f32[4,64,256]{2,1,0:T(8,128)S(1)} fusion(f32[4,64,256]{2,1,0:T(8,128)S(1)} %broadcast_in_dim.16, s32[64]{0:T(128)S(1)} %fusion.137, f32[64]{0:T(128)S(1)} %get-tuple-element.14), kind=kCustom, calls=%fused_computation | custom fusion | flops 64 | bytes 1536 | tf_op jit(solution)/shard_map/scatter-add | solution.py:79
  30.7 1.0 constant_dynamic-update-slice_fusion.2
  31.9 1.0 constant_dynamic-update-slice_fusion
  33.1 0.6 fusion.6
  33.8 0.6 fusion.9
  34.3 0.4 copy-done.1
  34.8 0.6 copy-done.4
  35.3 0.4 divide_bitcast_fusion.3
  35.9 0.2 fusion
  36.3 4.0 %collective-permute-start.2 = (f32[1,2,3,1,64,256]{5,4,3,1,2,0:T(8,128)S(1)}, f32[1,2,3,1,64,256]{5,4,3,1,2,0:T(8,128)S(1)}, u32[]{:S(2)}, u32[]{:S(2)}) collective-permute-start(f32[1,2,3,1,64,256]{5,4,3,1,2,0:T(8,128)S(1)} %copy.52), channel_id=1, source_target_pairs={{0,1},{1,2},{2,3},{3,4},{4,5},{5,6},{6,7},{7,8},{8,9},{9,10},{10,1... | collective-permute-start | bytes 1179656 | tf_op jit(solution)/shard_map/ppermute | solution.py:19
  40.3 1.3 collective-permute-start.3
  41.6 3.1 %collective-permute-done.4 = f32[1,2,3,1,64,256]{5,4,3,1,2,0:T(8,128)} collective-permute-done((f32[1,2,3,1,64,256]{5,4,3,1,2,0:T(8,128)}, f32[1,2,3,1,64,256]{5,4,3,1,2,0:T(8,128)}, u32[]{:S(2)}, u32[]{:S(2)}) %collective-permute-start.4) | collective-permute-done | bytes 393248 | tf_op jit(solution)/shard_map/ppermute | solution.py:19
  44.7 1.4 pad_maximum_fusion
  46.1 0.3 slice_bitcast_fusion.4
  46.4 5.5 %collective-permute-done.2 = f32[1,2,3,1,64,256]{5,4,3,1,2,0:T(8,128)S(1)} collective-permute-done((f32[1,2,3,1,64,256]{5,4,3,1,2,0:T(8,128)S(1)}, f32[1,2,3,1,64,256]{5,4,3,1,2,0:T(8,128)S(1)}, u32[]{:S(2)}, u32[]{:S(2)}) %collective-permute-start.2) | collective-permute-done | bytes 393248 | tf_op jit(solution)/shard_map/ppermute | solution.py:19
  52.2 5.0 %collective-permute-done.3 = f32[1,2,3,1,64,256]{5,4,3,1,2,0:T(8,128)S(1)} collective-permute-done((f32[1,2,3,1,64,256]{5,4,3,1,2,0:T(8,128)S(1)}, f32[1,2,3,1,64,256]{5,4,3,1,2,0:T(8,128)S(1)}, u32[]{:S(2)}, u32[]{:S(2)}) %collective-permute-start.3) | collective-permute-done | bytes 393248 | tf_op jit(solution)/shard_map/ppermute | solution.py:21
  57.2 0.3 slice_bitcast_fusion.9
  57.4 1.4 fusion.30
  58.9 0.5 fusion.33
  59.4 0.5 fusion.21
  60.0 0.5 divide_bitcast_fusion.1
  60.6 0.9 copy-done.6
  61.6 0.5 copy_subtract_fusion
  62.1 0.5 fusion.102
  62.9 5.8 %collective-permute-start.6 = (f32[1,2,3,1,64,256]{5,4,3,1,2,0:T(8,128)S(1)}, f32[1,2,3,1,64,256]{5,4,3,1,2,0:T(8,128)S(1)}, u32[]{:S(2)}, u32[]{:S(2)}) collective-permute-start(f32[1,2,3,1,64,256]{5,4,3,1,2,0:T(8,128)S(1)} %get-tuple-element.29), channel_id=1, source_target_pairs={{0,1},{1,2},{2,3},{3,4},{4,5},{5,6},{6,7},{7,8},{8,9},{9,10},{10,1... | collective-permute-start | bytes 1179656 | tf_op jit(solution)/shard_map/ppermute | solution.py:19
  68.7 0.4 fusion.1
  69.1 1.5 collective-permute-start.7
  70.6 0.2 fusion.2
  70.8 2.6 collective-permute-done.6
  73.7 15.4 %collective-permute-done.7 = f32[1,2,3,1,64,256]{5,4,3,1,2,0:T(8,128)S(1)} collective-permute-done((f32[1,2,3,1,64,256]{5,4,3,1,2,0:T(8,128)S(1)}, f32[1,2,3,1,64,256]{5,4,3,1,2,0:T(8,128)S(1)}, u32[]{:S(2)}, u32[]{:S(2)}) %collective-permute-start.7) | collective-permute-done | bytes 393248 | tf_op jit(solution)/shard_map/ppermute | solution.py:21
  89.1 0.3 slice_bitcast_fusion.1
  89.4 0.6 fusion.42
  90.0 0.5 fusion.45
  90.6 0.5 add_divide_fusion
  91.3 0.4 fusion.3
  91.7 0.3 fusion.108
  92.1 0.8 pad_maximum_fusion.9
  92.9 168.2 %all-reduce.51.cloned.1.call-done = f32[2,4,64,256]{3,2,1,0:T(8,128)} async-done(((f32[2,4,64,256]{3,2,1,0:T(8,128)}), f32[2,4,64,256]{3,2,1,0:T(8,128)}) %all-reduce.51.cloned.1.call-update) | async-done | bytes 524304 | tf_op jit(solution)/shard_map/psum | solution.py:133
  261.1 1.5 constant_dynamic-slice_fusion
  (41 shorter events, 2.3 us)
Async XLA Ops:
  7.2 8.9 %copy-start.3 = (bf16[1,2,3,4,64,256]{5,4,3,2,1,0:T(8,128)(2,1)S(1)}, bf16[1,2,3,4,64,256]{5,4,3,2,1,0:T(8,128)(2,1)}, u32[]{:S(2)}) copy-start(bf16[1,2,3,4,64,256]{5,4,3,2,1,0:T(8,128)(2,1)} %param.12) | copy-start | bytes 2359300
  7.2 253.9 %all-reduce.51.cloned.1.call-start = ((), (), s32[]{:S(2)}) async-start(), calls=%async_computation | async-start | bytes 1048576 | tf_op jit(solution)/shard_map/psum | solution.py:133
  9.2 21.5 %collective-permute-start = (f32[1,2,3,1,64,256]{5,4,3,1,2,0:T(8,128)}, f32[1,2,3,1,64,256]{5,4,3,1,2,0:T(8,128)}, u32[]{:S(2)}, u32[]{:S(2)}) collective-permute-start(f32[1,2,3,1,64,256]{5,4,3,1,2,0:T(8,128)} %copy.50), channel_id=1, source_target_pairs={{0,1},{1,2},{2,3},{3,4},{4,5},{5,6},{6,7},{7,8},{8,9},{9,10},{10,1... | collective-permute-start | bytes 1179656 | tf_op jit(solution)/shard_map/ppermute | solution.py:19
  14.7 9.3 %copy-start.7 = (s32[64]{0:T(128)S(1)}, s32[64]{0:T(128)}, u32[]{:S(2)}) copy-start(s32[64]{0:T(128)} %param.15) | copy-start | bytes 772
  14.7 9.3 %copy-start = (bf16[1,2,3,4,64,256]{5,4,3,2,1,0:T(8,128)(2,1)S(1)}, bf16[1,2,3,4,64,256]{5,4,3,2,1,0:T(8,128)(2,1)}, u32[]{:S(2)}) copy-start(bf16[1,2,3,4,64,256]{5,4,3,2,1,0:T(8,128)(2,1)} %param.11) | copy-start | bytes 2359300
  14.7 17.2 %collective-permute-start.1 = (f32[1,2,3,1,64,256]{5,4,3,1,2,0:T(8,128)}, f32[1,2,3,1,64,256]{5,4,3,1,2,0:T(8,128)}, u32[]{:S(2)}, u32[]{:S(2)}) collective-permute-start(f32[1,2,3,1,64,256]{5,4,3,1,2,0:T(8,128)} %copy.51), channel_id=1, source_target_pairs={{1,0},{2,1},{3,2},{4,3},{5,4},{6,5},{7,6},{8,7},{9,8},{10,9},{11,1... | collective-permute-start | bytes 1179656 | tf_op jit(solution)/shard_map/ppermute | solution.py:21
  17.3 27.4 %collective-permute-start.4 = (f32[1,2,3,1,64,256]{5,4,3,1,2,0:T(8,128)}, f32[1,2,3,1,64,256]{5,4,3,1,2,0:T(8,128)}, u32[]{:S(2)}, u32[]{:S(2)}) collective-permute-start(f32[1,2,3,1,64,256]{5,4,3,1,2,0:T(8,128)} %get-tuple-element.30), channel_id=1, source_target_pairs={{0,1},{1,2},{2,3},{3,4},{4,5},{5,6},{6,7},{7,8},{8,9},{9,10},{10,1... | collective-permute-start | bytes 1179656 | tf_op jit(solution)/shard_map/ppermute | solution.py:19
  22.0 22.7 %collective-permute-start.5 = (f32[1,2,3,1,64,256]{5,4,3,1,2,0:T(8,128)}, f32[1,2,3,1,64,256]{5,4,3,1,2,0:T(8,128)}, u32[]{:S(2)}, u32[]{:S(2)}) collective-permute-start(f32[1,2,3,1,64,256]{5,4,3,1,2,0:T(8,128)} %get-tuple-element.31), channel_id=1, source_target_pairs={{1,0},{2,1},{3,2},{4,3},{5,4},{6,5},{7,6},{8,7},{9,8},{10,9},{11,1... | collective-permute-start | bytes 1179656 | tf_op jit(solution)/shard_map/ppermute | solution.py:21
  33.7 1.0 copy-start.1
  33.7 1.0 copy-start.2
  33.8 1.6 copy-start.4
  36.3 15.6 %collective-permute-start.2 = (f32[1,2,3,1,64,256]{5,4,3,1,2,0:T(8,128)S(1)}, f32[1,2,3,1,64,256]{5,4,3,1,2,0:T(8,128)S(1)}, u32[]{:S(2)}, u32[]{:S(2)}) collective-permute-start(f32[1,2,3,1,64,256]{5,4,3,1,2,0:T(8,128)S(1)} %copy.52), channel_id=1, source_target_pairs={{0,1},{1,2},{2,3},{3,4},{4,5},{5,6},{6,7},{7,8},{8,9},{9,10},{10,1... | collective-permute-start | bytes 1179656 | tf_op jit(solution)/shard_map/ppermute | solution.py:19
  40.3 16.9 %collective-permute-start.3 = (f32[1,2,3,1,64,256]{5,4,3,1,2,0:T(8,128)S(1)}, f32[1,2,3,1,64,256]{5,4,3,1,2,0:T(8,128)S(1)}, u32[]{:S(2)}, u32[]{:S(2)}) collective-permute-start(f32[1,2,3,1,64,256]{5,4,3,1,2,0:T(8,128)S(1)} %copy.53), channel_id=1, source_target_pairs={{1,0},{2,1},{3,2},{4,3},{5,4},{6,5},{7,6},{8,7},{9,8},{10,9},{11,1... | collective-permute-start | bytes 1179656 | tf_op jit(solution)/shard_map/ppermute | solution.py:21
  60.4 1.1 copy-start.6
  62.9 10.5 %collective-permute-start.6 = (f32[1,2,3,1,64,256]{5,4,3,1,2,0:T(8,128)S(1)}, f32[1,2,3,1,64,256]{5,4,3,1,2,0:T(8,128)S(1)}, u32[]{:S(2)}, u32[]{:S(2)}) collective-permute-start(f32[1,2,3,1,64,256]{5,4,3,1,2,0:T(8,128)S(1)} %get-tuple-element.29), channel_id=1, source_target_pairs={{0,1},{1,2},{2,3},{3,4},{4,5},{5,6},{6,7},{7,8},{8,9},{9,10},{10,1... | collective-permute-start | bytes 1179656 | tf_op jit(solution)/shard_map/ppermute | solution.py:19
  69.1 22.6 %copy-start.5 = (f32[1,2,3,4,64,256]{5,4,3,2,1,0:T(8,128)}, f32[1,2,3,4,64,256]{5,4,3,2,1,0:T(8,128)S(1)}, u32[]{:S(2)}) copy-start(f32[1,2,3,4,64,256]{5,4,3,2,1,0:T(8,128)S(1)} %fusion.1) | copy-start | bytes 4718596
  69.1 20.0 %collective-permute-start.7 = (f32[1,2,3,1,64,256]{5,4,3,1,2,0:T(8,128)S(1)}, f32[1,2,3,1,64,256]{5,4,3,1,2,0:T(8,128)S(1)}, u32[]{:S(2)}, u32[]{:S(2)}) collective-permute-start(f32[1,2,3,1,64,256]{5,4,3,1,2,0:T(8,128)S(1)} %get-tuple-element.28), channel_id=1, source_target_pairs={{1,0},{2,1},{3,2},{4,3},{5,4},{6,5},{7,6},{8,7},{9,8},{10,9},{11,1... | collective-permute-start | bytes 1179656 | tf_op jit(solution)/shard_map/ppermute | solution.py:21
Sparse Core Ops, SparseCore 0:
  93.0 168.0 all-reduce.50
where the time goes:
time: 270 us; the launch traced here: 269 us
  waiting for transfers between devices  200 us (74%)
  starting transfers between devices  24.8 us (9%)
  other arithmetic  18.7 us (7%)
  between operations  15.8 us (6%)
  local copies, waits for them, and re-layouts  10.3 us (4%)
    psum x1, waiting for transfers between devices, on_device(): summed = lax.psum(local_grad, 'freq')  168 us
    ppermute x4, waiting for transfers between devices, padded_2(): lax.ppermute(head, axis, [((i + 1) % count, i) for i in range(ends)])  20.4 us
    ppermute x4, starting transfers between devices, padded_2(): lax.ppermute(tail, axis, [(i, (i + 1) % count) for i in range(ends)])  19.3 us
    ppermute x4, waiting for transfers between devices, padded_2(): lax.ppermute(tail, axis, [(i, (i + 1) % count) for i in range(ends)])  11.2 us
    ppermute x4, starting transfers between devices, padded_2(): lax.ppermute(head, axis, [((i + 1) % count, i) for i in range(ends)])  5.46 us
  transfers between devices with their start and end apart: 9, of which 6 were waited for; matrix products, arithmetic and copies ran while one was open for 6% of the time, Pallas kernels for 0%

commit v1 on v0

--- a/solution.py
+++ b/solution.py
@@ -130,7 +130,7 @@
     for sweep in range(ITERS):
         adjoint = local_sweep(adjoint, adjoint_rhs, sig_pair, wave_scale, inside_pad)
     local_grad = gradient_terms(efield, adjoint, wave_scale)
-    summed = lax.psum(local_grad, "freq")
+    summed = jnp.sum(lax.all_gather(local_grad, "freq"), axis=0)
     share_rows = size_y // lax.axis_size("freq")
     gradient = lax.dynamic_slice_in_dim(summed, lax.axis_index("freq") * share_rows, share_rows, 2)
     return (gradient, efield)

time: 270 us -> 208 us (0.77)
  waiting for transfers between devices: 200 us -> 134 us
  other arithmetic: 18.7 us -> 23.4 us
    psum x1 -> x0, waiting for transfers between devices: 168 us -> none  [on_device(): summed = lax.psum(local_grad, 'freq')]
    all_gather x0 -> x1, waiting for transfers between devices: none -> 103 us  [on_device(): summed = jnp.sum(lax.all_gather(local_grad, 'freq'), axis=0)]
    reduce_sum x0 -> x1, other arithmetic: none -> 4.01 us  [on_device(): summed = jnp.sum(lax.all_gather(local_grad, 'freq'), axis=0)]
  transfers between devices with their start and end apart: 9 -> 9, of which waited for: 6 -> 6; matrix products, arithmetic and copies ran while one was open for 6% -> 7% of each run, Pallas kernels for 0% -> 0%
where the time goes in v1:
time: 208 us
  waiting for transfers between devices  134 us (64%)
  starting transfers between devices  24.8 us (12%)
  other arithmetic  23.4 us (11%)
  between operations  15.8 us (8%)
  local copies, waits for them, and re-layouts  9.33 us (4%)
    all_gather x1, waiting for transfers between devices, on_device(): summed = jnp.sum(lax.all_gather(local_grad, 'freq'), axis=0)  103 us
    ppermute x4, waiting for transfers between devices, padded_2(): lax.ppermute(head, axis, [((i + 1) % count, i) for i in range(ends)])  20.5 us
    ppermute x4, starting transfers between devices, padded_2(): lax.ppermute(tail, axis, [(i, (i + 1) % count) for i in range(ends)])  19.3 us
    ppermute x4, waiting for transfers between devices, padded_2(): lax.ppermute(tail, axis, [(i, (i + 1) % count) for i in range(ends)])  11 us
    ppermute x4, starting transfers between devices, padded_2(): lax.ppermute(head, axis, [((i + 1) % count, i) for i in range(ends)])  5.46 us
    unnamed x23, local copies, waits for them, and re-layouts  4.64 us
    scatter-add x1, other arithmetic, make_source(): counts.at[jnp.clip(cell_x, 0, slab_width - 1), cell_y, cell_z].add(weights)  4.6 us
  transfers between devices with their start and end apart: 9, of which 6 were waited for; matrix products, arithmetic and copies ran while one was open for 7% of the time, Pallas kernels for 0%

profile of v1, /device:TPU:1, one launch (start us, length us, event | category | flops | bytes accessed | tf_op | source)
XLA Modules:
  0.0 207.7 jit_solution(2720383016536498574)
XLA Ops:
  7.2 1.2 fusion.149
  8.4 0.8 copy.83
  9.2 4.7 %collective-permute-start = (f32[1,2,3,1,64,256]{5,4,3,1,2,0:T(8,128)}, f32[1,2,3,1,64,256]{5,4,3,1,2,0:T(8,128)}, u32[]{:S(2)}, u32[]{:S(2)}) collective-permute-start(f32[1,2,3,1,64,256]{5,4,3,1,2,0:T(8,128)} %copy.83), channel_id=1, source_target_pairs={{0,1},{1,2},{2,3},{3,4},{4,5},{5,6},{6,7},{7,8},{8,9},{9,10},{10,1... | collective-permute-start | bytes 1179656 | tf_op jit(solution)/shard_map/ppermute | solution.py:19
  13.9 0.8 copy.84
  14.7 1.4 collective-permute-start.1
  16.3 1.0 fusion.147
  17.3 4.7 %collective-permute-start.4 = (f32[1,2,3,1,64,256]{5,4,3,1,2,0:T(8,128)}, f32[1,2,3,1,64,256]{5,4,3,1,2,0:T(8,128)}, u32[]{:S(2)}, u32[]{:S(2)}) collective-permute-start(f32[1,2,3,1,64,256]{5,4,3,1,2,0:T(8,128)} %get-tuple-element.30), channel_id=1, source_target_pairs={{0,1},{1,2},{2,3},{3,4},{4,5},{5,6},{6,7},{7,8},{8,9},{9,10},{10,1... | collective-permute-start | bytes 1179656 | tf_op jit(solution)/shard_map/ppermute | solution.py:19
  22.0 1.3 collective-permute-start.5
  24.0 1.3 convert_element_type.71
  26.0 4.6 %scatter_fusion = f32[4,64,256]{2,1,0:T(8,128)S(1)} fusion(f32[4,64,256]{2,1,0:T(8,128)S(1)} %broadcast_in_dim.16, s32[64]{0:T(128)S(1)} %fusion.137, f32[64]{0:T(128)S(1)} %get-tuple-element.14), kind=kCustom, calls=%fused_computation | custom fusion | flops 64 | bytes 1536 | tf_op jit(solution)/shard_map/scatter-add | solution.py:79
  30.7 1.0 constant_dynamic-update-slice_fusion.2
  31.9 1.0 constant_dynamic-update-slice_fusion
  33.1 0.6 fusion.6
  33.8 0.6 fusion.9
  34.3 0.4 copy-done.1
  34.8 0.6 copy-done.4
  35.3 0.4 divide_bitcast_fusion.3
  35.9 0.3 fusion
  36.3 4.0 %collective-permute-start.2 = (f32[1,2,3,1,64,256]{5,4,3,1,2,0:T(8,128)S(1)}, f32[1,2,3,1,64,256]{5,4,3,1,2,0:T(8,128)S(1)}, u32[]{:S(2)}, u32[]{:S(2)}) collective-permute-start(f32[1,2,3,1,64,256]{5,4,3,1,2,0:T(8,128)S(1)} %copy.85), channel_id=1, source_target_pairs={{0,1},{1,2},{2,3},{3,4},{4,5},{5,6},{6,7},{7,8},{8,9},{9,10},{10,1... | collective-permute-start | bytes 1179656 | tf_op jit(solution)/shard_map/ppermute | solution.py:19
  40.4 1.3 collective-permute-start.3
  41.6 3.0 %collective-permute-done.4 = f32[1,2,3,1,64,256]{5,4,3,1,2,0:T(8,128)} collective-permute-done((f32[1,2,3,1,64,256]{5,4,3,1,2,0:T(8,128)}, f32[1,2,3,1,64,256]{5,4,3,1,2,0:T(8,128)}, u32[]{:S(2)}, u32[]{:S(2)}) %collective-permute-start.4) | collective-permute-done | bytes 393248 | tf_op jit(solution)/shard_map/ppermute | solution.py:19
  44.7 1.4 pad_maximum_fusion
  46.1 0.3 slice_bitcast_fusion.4
  46.4 5.5 %collective-permute-done.2 = f32[1,2,3,1,64,256]{5,4,3,1,2,0:T(8,128)S(1)} collective-permute-done((f32[1,2,3,1,64,256]{5,4,3,1,2,0:T(8,128)S(1)}, f32[1,2,3,1,64,256]{5,4,3,1,2,0:T(8,128)S(1)}, u32[]{:S(2)}, u32[]{:S(2)}) %collective-permute-start.2) | collective-permute-done | bytes 393248 | tf_op jit(solution)/shard_map/ppermute | solution.py:19
  51.9 0.2 constant_dynamic-update-slice_fusion.4
  52.2 5.0 %collective-permute-done.3 = f32[1,2,3,1,64,256]{5,4,3,1,2,0:T(8,128)S(1)} collective-permute-done((f32[1,2,3,1,64,256]{5,4,3,1,2,0:T(8,128)S(1)}, f32[1,2,3,1,64,256]{5,4,3,1,2,0:T(8,128)S(1)}, u32[]{:S(2)}, u32[]{:S(2)}) %collective-permute-start.3) | collective-permute-done | bytes 393248 | tf_op jit(solution)/shard_map/ppermute | solution.py:21
  57.4 1.5 fusion.30
  58.9 0.5 fusion.33
  59.5 0.5 fusion.21
  60.0 0.5 divide_bitcast_fusion.1
  60.8 0.9 copy-done.6
  61.7 0.6 copy_subtract_fusion
  62.2 0.5 fusion.102
  63.1 5.8 %collective-permute-start.6 = (f32[1,2,3,1,64,256]{5,4,3,1,2,0:T(8,128)S(1)}, f32[1,2,3,1,64,256]{5,4,3,1,2,0:T(8,128)S(1)}, u32[]{:S(2)}, u32[]{:S(2)}) collective-permute-start(f32[1,2,3,1,64,256]{5,4,3,1,2,0:T(8,128)S(1)} %get-tuple-element.29), channel_id=1, source_target_pairs={{0,1},{1,2},{2,3},{3,4},{4,5},{5,6},{6,7},{7,8},{8,9},{9,10},{10,1... | collective-permute-start | bytes 1179656 | tf_op jit(solution)/shard_map/ppermute | solution.py:19
  68.9 0.4 fusion.1
  69.4 1.5 collective-permute-start.7
  70.9 0.3 fusion.2
  71.1 2.5 %collective-permute-done.6 = f32[1,2,3,1,64,256]{5,4,3,1,2,0:T(8,128)S(1)} collective-permute-done((f32[1,2,3,1,64,256]{5,4,3,1,2,0:T(8,128)S(1)}, f32[1,2,3,1,64,256]{5,4,3,1,2,0:T(8,128)S(1)}, u32[]{:S(2)}, u32[]{:S(2)}) %collective-permute-start.6) | collective-permute-done | bytes 393248 | tf_op jit(solution)/shard_map/ppermute | solution.py:19
  73.9 15.5 %collective-permute-done.7 = f32[1,2,3,1,64,256]{5,4,3,1,2,0:T(8,128)S(1)} collective-permute-done((f32[1,2,3,1,64,256]{5,4,3,1,2,0:T(8,128)S(1)}, f32[1,2,3,1,64,256]{5,4,3,1,2,0:T(8,128)S(1)}, u32[]{:S(2)}, u32[]{:S(2)}) %collective-permute-start.7) | collective-permute-done | bytes 393248 | tf_op jit(solution)/shard_map/ppermute | solution.py:21
  89.6 0.7 fusion.42
  90.3 0.5 fusion.45
  90.8 0.6 add_divide_fusion
  91.6 0.4 fusion.3
  92.1 0.3 fusion.108
  92.4 0.9 pad_maximum_fusion.9
  93.4 102.9 %all-gather.3.cloned.1.call-done = f32[32,4,64,256]{3,2,1,0:T(8,128)} async-done(((f32[2,4,64,256]{3,2,1,0:T(8,128)}), f32[32,4,64,256]{3,2,1,0:T(8,128)}) %all-gather.3.cloned.1.call-update) | async-done | bytes 8388624 | tf_op jit(solution)/shard_map/all_gather | solution.py:133
  196.2 4.0 %reduce_sum.8 = f32[2,4,64,256]{3,2,1,0:T(8,128)S(1)} reduce(f32[16,2,4,64,256]{4,3,2,1,0:T(8,128)} %bitcast.231, f32[]{:T(128)} %constant.71.clone.1), dimensions={0}, to_apply=%region_1.2 | reduce | flops 1966080 | bytes 8912900 | tf_op jit(solution)/shard_map/reduce_sum | solution.py:133
  200.2 0.6 constant_dynamic-slice_fusion
  (42 shorter events, 2.6 us)
Async XLA Ops:
  7.2 8.9 %copy-start.3 = (bf16[1,2,3,4,64,256]{5,4,3,2,1,0:T(8,128)(2,1)S(1)}, bf16[1,2,3,4,64,256]{5,4,3,2,1,0:T(8,128)(2,1)}, u32[]{:S(2)}) copy-start(bf16[1,2,3,4,64,256]{5,4,3,2,1,0:T(8,128)(2,1)} %param.12) | copy-start | bytes 2359300
  7.2 189.1 %all-gather.3.cloned.1.call-start = ((), (), s32[]{:S(2)}) async-start(), calls=%async_computation | async-start | bytes 8912896 | tf_op jit(solution)/shard_map/all_gather | solution.py:133
  9.2 21.5 %collective-permute-start = (f32[1,2,3,1,64,256]{5,4,3,1,2,0:T(8,128)}, f32[1,2,3,1,64,256]{5,4,3,1,2,0:T(8,128)}, u32[]{:S(2)}, u32[]{:S(2)}) collective-permute-start(f32[1,2,3,1,64,256]{5,4,3,1,2,0:T(8,128)} %copy.83), channel_id=1, source_target_pairs={{0,1},{1,2},{2,3},{3,4},{4,5},{5,6},{6,7},{7,8},{8,9},{9,10},{10,1... | collective-permute-start | bytes 1179656 | tf_op jit(solution)/shard_map/ppermute | solution.py:19
  14.7 9.3 %copy-start.7 = (s32[64]{0:T(128)S(1)}, s32[64]{0:T(128)}, u32[]{:S(2)}) copy-start(s32[64]{0:T(128)} %param.15) | copy-start | bytes 772
  14.7 9.3 %copy-start = (bf16[1,2,3,4,64,256]{5,4,3,2,1,0:T(8,128)(2,1)S(1)}, bf16[1,2,3,4,64,256]{5,4,3,2,1,0:T(8,128)(2,1)}, u32[]{:S(2)}) copy-start(bf16[1,2,3,4,64,256]{5,4,3,2,1,0:T(8,128)(2,1)} %param.11) | copy-start | bytes 2359300
  14.7 17.2 %collective-permute-start.1 = (f32[1,2,3,1,64,256]{5,4,3,1,2,0:T(8,128)}, f32[1,2,3,1,64,256]{5,4,3,1,2,0:T(8,128)}, u32[]{:S(2)}, u32[]{:S(2)}) collective-permute-start(f32[1,2,3,1,64,256]{5,4,3,1,2,0:T(8,128)} %copy.84), channel_id=1, source_target_pairs={{1,0},{2,1},{3,2},{4,3},{5,4},{6,5},{7,6},{8,7},{9,8},{10,9},{11,1... | collective-permute-start | bytes 1179656 | tf_op jit(solution)/shard_map/ppermute | solution.py:21
  17.3 27.4 %collective-permute-start.4 = (f32[1,2,3,1,64,256]{5,4,3,1,2,0:T(8,128)}, f32[1,2,3,1,64,256]{5,4,3,1,2,0:T(8,128)}, u32[]{:S(2)}, u32[]{:S(2)}) collective-permute-start(f32[1,2,3,1,64,256]{5,4,3,1,2,0:T(8,128)} %get-tuple-element.30), channel_id=1, source_target_pairs={{0,1},{1,2},{2,3},{3,4},{4,5},{5,6},{6,7},{7,8},{8,9},{9,10},{10,1... | collective-permute-start | bytes 1179656 | tf_op jit(solution)/shard_map/ppermute | solution.py:19
  22.0 22.7 %collective-permute-start.5 = (f32[1,2,3,1,64,256]{5,4,3,1,2,0:T(8,128)}, f32[1,2,3,1,64,256]{5,4,3,1,2,0:T(8,128)}, u32[]{:S(2)}, u32[]{:S(2)}) collective-permute-start(f32[1,2,3,1,64,256]{5,4,3,1,2,0:T(8,128)} %get-tuple-element.31), channel_id=1, source_target_pairs={{1,0},{2,1},{3,2},{4,3},{5,4},{6,5},{7,6},{8,7},{9,8},{10,9},{11,1... | collective-permute-start | bytes 1179656 | tf_op jit(solution)/shard_map/ppermute | solution.py:21
  33.7 1.0 copy-start.1
  33.7 1.0 copy-start.2
  33.8 1.6 copy-start.4
  36.3 15.6 %collective-permute-start.2 = (f32[1,2,3,1,64,256]{5,4,3,1,2,0:T(8,128)S(1)}, f32[1,2,3,1,64,256]{5,4,3,1,2,0:T(8,128)S(1)}, u32[]{:S(2)}, u32[]{:S(2)}) collective-permute-start(f32[1,2,3,1,64,256]{5,4,3,1,2,0:T(8,128)S(1)} %copy.85), channel_id=1, source_target_pairs={{0,1},{1,2},{2,3},{3,4},{4,5},{5,6},{6,7},{7,8},{8,9},{9,10},{10,1... | collective-permute-start | bytes 1179656 | tf_op jit(solution)/shard_map/ppermute | solution.py:19
  40.4 16.9 %collective-permute-start.3 = (f32[1,2,3,1,64,256]{5,4,3,1,2,0:T(8,128)S(1)}, f32[1,2,3,1,64,256]{5,4,3,1,2,0:T(8,128)S(1)}, u32[]{:S(2)}, u32[]{:S(2)}) collective-permute-start(f32[1,2,3,1,64,256]{5,4,3,1,2,0:T(8,128)S(1)} %copy.86), channel_id=1, source_target_pairs={{1,0},{2,1},{3,2},{4,3},{5,4},{6,5},{7,6},{8,7},{9,8},{10,9},{11,1... | collective-permute-start | bytes 1179656 | tf_op jit(solution)/shard_map/ppermute | solution.py:21
  60.5 1.1 copy-start.6
  63.1 10.5 %collective-permute-start.6 = (f32[1,2,3,1,64,256]{5,4,3,1,2,0:T(8,128)S(1)}, f32[1,2,3,1,64,256]{5,4,3,1,2,0:T(8,128)S(1)}, u32[]{:S(2)}, u32[]{:S(2)}) collective-permute-start(f32[1,2,3,1,64,256]{5,4,3,1,2,0:T(8,128)S(1)} %get-tuple-element.29), channel_id=1, source_target_pairs={{0,1},{1,2},{2,3},{3,4},{4,5},{5,6},{6,7},{7,8},{8,9},{9,10},{10,1... | collective-permute-start | bytes 1179656 | tf_op jit(solution)/shard_map/ppermute | solution.py:19
  69.4 22.7 %copy-start.5 = (f32[1,2,3,4,64,256]{5,4,3,2,1,0:T(8,128)}, f32[1,2,3,4,64,256]{5,4,3,2,1,0:T(8,128)S(1)}, u32[]{:S(2)}) copy-start(f32[1,2,3,4,64,256]{5,4,3,2,1,0:T(8,128)S(1)} %fusion.1) | copy-start | bytes 4718596
  69.4 20.0 %collective-permute-start.7 = (f32[1,2,3,1,64,256]{5,4,3,1,2,0:T(8,128)S(1)}, f32[1,2,3,1,64,256]{5,4,3,1,2,0:T(8,128)S(1)}, u32[]{:S(2)}, u32[]{:S(2)}) collective-permute-start(f32[1,2,3,1,64,256]{5,4,3,1,2,0:T(8,128)S(1)} %get-tuple-element.28), channel_id=1, source_target_pairs={{1,0},{2,1},{3,2},{4,3},{5,4},{6,5},{7,6},{8,7},{9,8},{10,9},{11,1... | collective-permute-start | bytes 1179656 | tf_op jit(solution)/shard_map/ppermute | solution.py:21
Sparse Core Ops, SparseCore 0:
  93.5 102.6 all-gather.2
